TPU v7x, 256 devices: a whole 4x4x8 slice. The times are simulated.
256 devices in a mesh: blk: 16 (over z, core), head: 4 (over x), dp: 4 (over y).
Axes of the slice: x: 4, y: 4, z: 8, core: 2. Of those that a mesh axis runs over, the one named last changes fastest.
Arguments:
- hidden: bfloat16 [49152, 3072], P(('dp', 'blk', 'head')), parts along dimension 0, may hold values from -36 to 36
- qkv_weight: bfloat16 [3, 3072, 1536], P(None, None, 'head'), may hold values from -0.109375 to 0.109375
- qkv_bias: bfloat16 [3, 1536], P(None, 'head'), may hold values from -3 to 3
- norm_gains: float32 [2, 128], replicated, may hold values from 0.25 to 1.75
- tile_lists: int32 [128, 12], P('dp'), parts along dimension 0, may hold values from 0 to 31, as said below
- tile_counts: int32 [128], P('dp'), parts along dimension 0, may hold values from 1 to 12
Outputs:
- attended: bfloat16 [49152, 1536], P(('dp', 'blk', 'head')), parts along dimension 0
There are 4 independent parts, one for each index of `dp`. A program takes and returns all parts, laid end to end along the dimension named above; an argument that names none is the same for every part. Nothing has to cross between parts.
Inputs may be any that keep to these rules, and one draw needn't show every extreme that they name: `tile_lists`: entries 0 to tile_counts[a] - 1 of row a name distinct tiles, tile a among them; later entries are arbitrary tile indices.
All inputs are finite; a program needn't handle non-finite values.
Results may differ from a plain program's by a relative error of at most 0.0034.
Values may be sent and summed in bfloat16 or wider, within the bound.
A program may use at most 64 MiB of HBM per device.

v0:
```python
import jax
import jax.numpy as jnp
from jax import lax
from jax.sharding import PartitionSpec as P

HD = 128
TILE = 384


def shifted(block, axis, distance):
    devices = range(lax.axis_size(axis))
    route = [(i - distance, i) for i in devices if i - distance in devices]
    return lax.ppermute(block, axis, route)


def norm_heads(values, gain, heads):
    rows = values.shape[0]
    split = values.reshape(rows, heads, HD)
    mean_sq = jnp.mean(split * split, axis=-1, keepdims=True)
    return (split * lax.rsqrt(mean_sq + 1e-06) * gain).reshape(rows, heads * HD)


def tile_mask(lists, counts, start, rows):
    key_tile = (start + jnp.arange(rows, dtype=jnp.int32)) // TILE
    live = jnp.arange(lists.shape[1], dtype=jnp.int32)[None, :] < counts[:, None]
    hits = (lists[:, :, None] == key_tile[None, None, :]) & live[:, :, None]
    return jnp.any(hits, axis=1)


def tile_terms(query, keys, values, mask, heads):
    count_q = query.shape[0]
    rows = keys.shape[0]
    query_h = query.reshape(count_q, heads, HD)
    keys_h = keys.reshape(rows, heads, HD)
    values_h = values.reshape(rows, heads, HD)
    score = jnp.einsum(
        "qhd,khd->hqk", query_h, keys_h, preferred_element_type=jnp.float32
    ) * HD ** (-0.5)
    score = score.reshape(heads, count_q // TILE, TILE, rows)
    weights = jnp.where(mask[None, :, None, :], jnp.exp(score), jnp.float32(0.0)).reshape(
        heads, count_q, rows
    )
    sums = jnp.sum(weights, axis=-1)
    terms = jnp.einsum(
        "hqk,khd->qhd", weights.astype(jnp.bfloat16), values_h, preferred_element_type=jnp.float32
    )
    return (sums, terms.reshape(count_q, heads * HD))


def add_block(state, query, lists, counts, keys, values, start, heads):
    total, numer = state
    mask = tile_mask(lists, counts, start, keys.shape[0])
    sums, terms = tile_terms(query, keys, values, mask, heads)
    return (total + sums, numer + terms)


def attend(state, query, lists, counts, keys, values, start, heads):
    return add_block(state, query, lists, counts, keys, values, start, heads)


def shards(hidden, qkv_weight, qkv_bias, norm_gains, tile_lists, tile_counts):
    heads = qkv_weight.shape[2] // HD
    piece = lax.all_gather(hidden, "head", axis=0, tiled=True)
    made = [
        jnp.dot(piece, qkv_weight[j], preferred_element_type=jnp.float32)
        + qkv_bias[j].astype(jnp.float32)
        for j in range(3)
    ]
    query_part = norm_heads(made[0], norm_gains[0], heads)
    key_part = norm_heads(made[1], norm_gains[1], heads)
    stacked = jnp.stack([query_part, key_part, made[2]]).astype(jnp.bfloat16)
    query = stacked[0]
    key_value = stacked[1:3]
    rows_blk = query.shape[0]
    tiles_here = rows_blk // TILE
    place = lax.axis_index("blk")
    lists = lax.dynamic_slice_in_dim(tile_lists, place * tiles_here, tiles_here, 0)
    counts = lax.dynamic_slice_in_dim(tile_counts, place * tiles_here, tiles_here, 0)
    state = (
        jnp.zeros((heads, rows_blk), jnp.float32),
        jnp.zeros((rows_blk, heads * HD), jnp.float32),
    )
    key_group = lists // tiles_here
    live = jnp.arange(lists.shape[1], dtype=jnp.int32)[None, :] < counts[:, None]
    ahead = jnp.max(jnp.where(live, key_group - place, 0))
    behind = jnp.max(jnp.where(live, place - key_group, 0))
    farthest = lax.pmax(jnp.stack([ahead, behind]), "blk")
    state = attend(state, query, lists, counts, key_value[0], key_value[1], place * rows_blk, heads)

    def turn(step, carry):
        current, above, below = carry
        above = shifted(above, "blk", -1)
        below = shifted(below, "blk", 1)
        current = attend(
            current, query, lists, counts, above[0], above[1], (place + step + 1) * rows_blk, heads
        )
        current = attend(
            current, query, lists, counts, below[0], below[1], (place - step - 1) * rows_blk, heads
        )
        return (current, above, below)

    steps = jnp.maximum(farthest[0], farthest[1])
    state, unused_above, unused_below = lax.fori_loop(0, steps, turn, (state, key_value, key_value))
    total, numer = state
    attended = (
        (numer.reshape(rows_blk, heads, HD) / total.T[:, :, None])
        .reshape(rows_blk, heads * HD)
        .astype(jnp.bfloat16)
    )
    return lax.all_to_all(attended, "head", split_axis=0, concat_axis=1, tiled=True)


def solution(mesh):
    return jax.shard_map(
        shards,
        mesh=mesh,
        in_specs=(
            P(("dp", "blk", "head"), None),
            P(None, None, "head"),
            P(None, "head"),
            P(),
            P("dp", None),
            P("dp"),
        ),
        out_specs=P(("dp", "blk", "head"), None),
        check_vma=False,
    )
```

profile of v0, /device:TPU:65, one launch (start us, length us, event | category | flops | bytes accessed | tf_op | source)
XLA Modules:
  0.0 199.9 jit_solution(13299230233405282443)
XLA Ops:
  8.9 1.3 pad_add_fusion
  10.2 12.0 %pmax.7 = s32[2]{0:T(128)S(1)} all-reduce(s32[2]{0:T(128)S(1)} %pad_add_fusion), channel_id=1, replica_groups=mesh['blk'=16,'head'=4,'dp'=4] {'blk'}, use_global_device_ids=true, to_apply=%region_6.7 | all-reduce | flops 2 | bytes 16 | tf_op jit(solution)/shard_map/pmax | solution.py:87
  22.6 1.6 copy.56
  27.2 39.2 %all-gather.2.cloned.1.call-done = bf16[768,3072]{1,0:T(8,128)(2,1)} async-done(((bf16[192,3072]{1,0:T(8,128)(2,1)}), bf16[768,3072]{1,0:T(8,128)(2,1)}) %all-gather.2.cloned.1.call-update) | async-done | bytes 4718608 | tf_op jit(solution)/shard_map/all_gather | solution.py:63
  66.3 5.1 %fusion.60 = (f32[768,384]{0,1:T(8,128)S(1)}, f32[768,384]{0,1:T(8,128)S(1)}) fusion(f32[384]{0:T(512)S(1)} %get-tuple-element.181, bf16[768,3072]{1,0:T(8,128)(2,1)} %all-gather.2.cloned.1.call-done, bf16[3,3072,384]{2,1,0:T(8,128)(2,1)} %param.9), kind=kOutput, calls=%fused_computation.93 | convolution fusion | flops 1812529152 | bytes 9438720 | tf_op jit(solution)/shard_map/dot_general | solution.py:65
  72.2 5.1 %fusion.59 = (f32[768,384]{0,1:T(8,128)S(1)}, f32[768,384]{0,1:T(8,128)S(1)}) fusion(f32[384]{0:T(512)} %get-tuple-element.180, bf16[768,3072]{1,0:T(8,128)(2,1)} %all-gather.2.cloned.1.call-done, bf16[3,3072,384]{2,1,0:T(8,128)(2,1)} %param.9), kind=kOutput, calls=%fused_computation.92 | convolution fusion | flops 1812529152 | bytes 9439232 | tf_op jit(solution)/shard_map/dot_general | solution.py:65
  79.6 5.1 %fusion.45 = bf16[768,384]{0,1:T(8,128)(2,1)S(1)} fusion(bf16[768,3072]{1,0:T(8,128)(2,1)} %all-gather.2.cloned.1.call-done, bf16[3,3072,384]{2,1,0:T(8,128)(2,1)} %param.9, f32[384]{0:T(512)} %get-tuple-element.179), kind=kOutput, calls=%fused_computation.53 | convolution fusion | flops 1812529152 | bytes 7669760 | tf_op jit(solution)/shard_map/dot_general | solution.py:65
  84.7 1.1 pad_maximum_fusion
  85.8 2.5 %copy.81 = bf16[2,768,384]{1,2,0:T(8,128)(2,1)} copy(bf16[2,768,384]{1,2,0:T(8,128)(2,1)} %pad_maximum_fusion) | data formatting | bytes 2359296
  88.4 2.5 %fusion.21 = (f32[3,768]{1,0:T(4,128)}, f32[3,768,768]{1,2,0:T(8,128)S(1)}) fusion(pred[768,768]{0,1:T(8,128)(4,1)S(1)} %copy-done.4, bf16[768,3,128]{0,2,1:T(8,128)(2,1)S(1)} %bitcast.138, bf16[768,3,128]{0,2,1:T(8,128)(2,1)S(1)} %bitcast.135), kind=kOutput, calls=%fused_computation.36 | convolution fusion | flops 458290944 | bytes 8856576 | tf_op jit(solution)/shard_map/qhd,khd->hqk/dot_general | solution.py:36
  91.0 2.6 %fusion.22 = f32[3,128,768]{2,1,0:T(8,128)} fusion(bf16[768,3,128]{0,2,1:T(8,128)(2,1)S(1)} %bitcast.143, f32[3,768,768]{1,2,0:T(8,128)S(1)} %get-tuple-element.223, pred[768,768]{0,1:T(8,128)(4,1)S(1)} %copy-done.4), kind=kOutput, calls=%fused_computation.37 | convolution fusion | flops 458293248 | bytes 9437184 | tf_op jit(solution)/shard_map/hqk,khd->qhd/dot_general | solution.py:44
  93.5 84.3 %while.19 = (s32[]{:T(128)}, f32[3,768]{1,0:T(4,128)}, f32[768,384]{0,1:T(8,128)}, bf16[2,768,384]{1,2,0:T(8,128)(2,1)}, bf16[2,768,384]{1,2,0:T(8,128)(2,1)}, /...) while((s32[]{:T(128)}, f32[3,768]{1,0:T(4,128)}, ...), condition=%wide.region_12.13_spmd, body=%wide.region_7.12_spmd.sunk | while | flops 1833884160 | bytes 78004824 | solution.py:103
  93.5 2.7 %collective-permute-start.1 = (bf16[2,768,384]{1,2,0:T(8,128)(2,1)}, bf16[2,768,384]{1,2,0:T(8,128)(2,1)S(1)}, u32[]{:S(2)}, u32[]{:S(2)}) collective-permute-start(bf16[2,768,384]{1,2,0:T(8,128)(2,1)} %get-tuple-element.328), channel_id=1, source_target_pairs={{16,0},{32,16},{48,32},{64,48},{80,64},{96,80},{112,96},{128,112},... | collective-permute-start | bytes 3538952 | tf_op jit(solution)/shard_map/while/body/ppermute | solution.py:13
  96.3 3.1 %collective-permute-start = (bf16[2,768,384]{1,2,0:T(8,128)(2,1)}, bf16[2,768,384]{1,2,0:T(8,128)(2,1)S(1)}, u32[]{:S(2)}, u32[]{:S(2)}) collective-permute-start(bf16[2,768,384]{1,2,0:T(8,128)(2,1)} %get-tuple-element.329), channel_id=1, source_target_pairs={{0,16},{16,32},{32,48},{48,64},{64,80},{80,96},{96,112},{112,128},... | collective-permute-start | bytes 3538952 | tf_op jit(solution)/shard_map/while/body/ppermute | solution.py:13
  99.8 1.6 copy.76
  101.5 1.0 copy.75
  102.5 9.3 %collective-permute-done.1 = bf16[2,768,384]{1,2,0:T(8,128)(2,1)S(1)} collective-permute-done((bf16[2,768,384]{1,2,0:T(8,128)(2,1)}, bf16[2,768,384]{1,2,0:T(8,128)(2,1)S(1)}, u32[]{:S(2)}, u32[]{:S(2)}) %collective-permute-start.1) | collective-permute-done | bytes 1179680 | tf_op jit(solution)/shard_map/while/body/ppermute | solution.py:13
  111.9 1.9 fusion.98
  113.8 1.6 fusion.100
  115.5 1.9 fusion.96
  117.5 1.5 fusion.99
  119.7 1.0 copy.90
  120.8 1.0 copy.91
  121.8 1.9 collective-permute-start.1
  123.7 3.6 %collective-permute-start = (bf16[2,768,384]{1,2,0:T(8,128)(2,1)}, bf16[2,768,384]{1,2,0:T(8,128)(2,1)S(1)}, u32[]{:S(2)}, u32[]{:S(2)}) collective-permute-start(bf16[2,768,384]{1,2,0:T(8,128)(2,1)} %get-tuple-element.329), channel_id=1, source_target_pairs={{0,16},{16,32},{32,48},{48,64},{64,80},{80,96},{96,112},{112,128},... | collective-permute-start | bytes 3538952 | tf_op jit(solution)/shard_map/while/body/ppermute | solution.py:13
  127.8 1.6 copy.76
  129.5 1.0 copy.75
  130.6 9.3 %collective-permute-done.1 = bf16[2,768,384]{1,2,0:T(8,128)(2,1)S(1)} collective-permute-done((bf16[2,768,384]{1,2,0:T(8,128)(2,1)}, bf16[2,768,384]{1,2,0:T(8,128)(2,1)S(1)}, u32[]{:S(2)}, u32[]{:S(2)}) %collective-permute-start.1) | collective-permute-done | bytes 1179680 | tf_op jit(solution)/shard_map/while/body/ppermute | solution.py:13
  139.9 1.9 fusion.98
  141.9 1.6 fusion.100
  143.6 1.9 fusion.96
  145.5 1.5 fusion.99
  147.8 1.0 copy.90
  148.8 1.0 copy.91
  149.8 1.9 collective-permute-start.1
  151.8 3.6 %collective-permute-start = (bf16[2,768,384]{1,2,0:T(8,128)(2,1)}, bf16[2,768,384]{1,2,0:T(8,128)(2,1)S(1)}, u32[]{:S(2)}, u32[]{:S(2)}) collective-permute-start(bf16[2,768,384]{1,2,0:T(8,128)(2,1)} %get-tuple-element.329), channel_id=1, source_target_pairs={{0,16},{16,32},{32,48},{48,64},{64,80},{80,96},{96,112},{112,128},... | collective-permute-start | bytes 3538952 | tf_op jit(solution)/shard_map/while/body/ppermute | solution.py:13
  155.8 1.6 copy.76
  157.5 1.0 copy.75
  158.6 9.3 %collective-permute-done.1 = bf16[2,768,384]{1,2,0:T(8,128)(2,1)S(1)} collective-permute-done((bf16[2,768,384]{1,2,0:T(8,128)(2,1)}, bf16[2,768,384]{1,2,0:T(8,128)(2,1)S(1)}, u32[]{:S(2)}, u32[]{:S(2)}) %collective-permute-start.1) | collective-permute-done | bytes 1179680 | tf_op jit(solution)/shard_map/while/body/ppermute | solution.py:13
  168.0 1.9 fusion.98
  169.9 1.6 fusion.100
  171.6 1.9 fusion.96
  173.5 1.5 fusion.99
  175.8 1.0 copy.90
  176.8 1.0 copy.91
  177.9 1.4 fusion.48
  179.5 12.7 %all_to_all.19 = bf16[4,192,384]{2,1,0:T(8,128)(2,1)S(1)} all-to-all(bf16[4,192,384]{2,1,0:T(8,128)(2,1)S(1)} %bitcast.132), channel_id=1, replica_groups=mesh['blk'=16,'head'=4,'dp'=4] {'head'}, dimensions={0} | all-to-all | bytes 1179648 | tf_op jit(solution)/shard_map/all_to_all | solution.py:110
  192.2 0.9 copy.72
  (101 shorter events, 12.1 us)
Async XLA Ops:
  6.5 0.7 copy-start
  6.5 19.4 %copy-start.9 = (bf16[3,384]{1,0:T(4,128)(2,1)S(1)}, bf16[3,384]{1,0:T(4,128)(2,1)}, u32[]{:S(2)}) copy-start(bf16[3,384]{1,0:T(4,128)(2,1)} %param.10) | copy-start | bytes 6916
  6.5 20.1 %copy-start.10 = (f32[2,128]{1,0:T(2,128)S(1)}, f32[2,128]{1,0:T(2,128)}, u32[]{:S(2)}) copy-start(f32[2,128]{1,0:T(2,128)} %param.11) | copy-start | bytes 3076
  6.5 59.8 %all-gather.2.cloned.1.call-start = ((), (), s32[]{:S(2)}) async-start(), calls=%async_computation.1 | async-start | bytes 5898240 | tf_op jit(solution)/shard_map/all_gather | solution.py:63
  8.2 14.2 %copy-start.11 = (s32[2]{0:T(128)}, s32[2]{0:T(128)S(1)}, u32[]{:S(2)}) copy-start(s32[2]{0:T(128)S(1)} %dynamic_slice.7) | copy-start | bytes 28
  85.8 2.7 %copy-start.4 = (pred[768,768]{0,1:T(8,128)(4,1)S(1)}, pred[768,768]{0,1:T(8,128)(4,1)}, u32[]{:S(2)}) copy-start(pred[768,768]{0,1:T(8,128)(4,1)} %copy.56) | copy-start | bytes 1769476
  88.4 2.5 %copy-start.5 = (bf16[768,384]{0,1:T(8,128)(2,1)}, bf16[768,384]{0,1:T(8,128)(2,1)S(1)}, u32[]{:S(2)}) copy-start(bf16[768,384]{0,1:T(8,128)(2,1)S(1)} %fusion.52) | copy-start | bytes 1769476
  91.0 2.6 %copy-start.12 = (s32[2]{0:T(128)S(1)}, s32[2]{0:T(128)}, u32[]{:S(2)}) copy-start(s32[2]{0:T(128)} %copy-done.11) | copy-start | bytes 28
  93.5 18.3 %collective-permute-start.1 = (bf16[2,768,384]{1,2,0:T(8,128)(2,1)}, bf16[2,768,384]{1,2,0:T(8,128)(2,1)S(1)}, u32[]{:S(2)}, u32[]{:S(2)}) collective-permute-start(bf16[2,768,384]{1,2,0:T(8,128)(2,1)} %get-tuple-element.328), channel_id=1, source_target_pairs={{16,0},{32,16},{48,32},{64,48},{80,64},{96,80},{112,96},{128,112},... | collective-permute-start | bytes 3538952 | tf_op jit(solution)/shard_map/while/body/ppermute | solution.py:13
  96.3 19.2 %collective-permute-start = (bf16[2,768,384]{1,2,0:T(8,128)(2,1)}, bf16[2,768,384]{1,2,0:T(8,128)(2,1)S(1)}, u32[]{:S(2)}, u32[]{:S(2)}) collective-permute-start(bf16[2,768,384]{1,2,0:T(8,128)(2,1)} %get-tuple-element.329), channel_id=1, source_target_pairs={{0,16},{16,32},{32,48},{48,64},{64,80},{80,96},{96,112},{112,128},... | collective-permute-start | bytes 3538952 | tf_op jit(solution)/shard_map/while/body/ppermute | solution.py:13
  102.5 9.4 %copy-start.3 = (pred[768,768]{0,1:T(8,128)(4,1)S(1)}, pred[768,768]{0,1:T(8,128)(4,1)}, u32[]{:S(2)}) copy-start(pred[768,768]{0,1:T(8,128)(4,1)} %copy.76) | copy-start | bytes 1769476 | tf_op jit(solution)/shard_map/while
  102.5 9.4 %copy-start.6 = (bf16[1,768,384]{1,2,0:T(8,128)(2,1)S(1)}, bf16[1,768,384]{1,2,0:T(8,128)(2,1)}, u32[]{:S(2)}) copy-start(bf16[1,768,384]{1,2,0:T(8,128)(2,1)} %get-tuple-element.347) | copy-start | bytes 1769476 | tf_op jit(solution)/shard_map/while
  117.4 1.6 copy-start.1
  119.0 0.7 copy-start.7
  119.4 2.5 %copy-start.2 = (f32[768,384]{0,1:T(8,128)}, f32[768,384]{0,1:T(8,128)S(1)}, u32[]{:S(2)}) copy-start(f32[768,384]{0,1:T(8,128)S(1)} %bitcast_add_fusion.3) | copy-start | bytes 3538948 | tf_op jit(solution)/shard_map/while
  119.7 2.1 %copy-start.8 = (f32[3,768]{1,0:T(4,128)}, f32[3,768]{1,0:T(4,128)S(1)}, u32[]{:S(2)}) copy-start(f32[3,768]{1,0:T(4,128)S(1)} %add_add_fusion.2) | copy-start | bytes 27652 | tf_op jit(solution)/shard_map/while
  121.8 18.0 %collective-permute-start.1 = (bf16[2,768,384]{1,2,0:T(8,128)(2,1)}, bf16[2,768,384]{1,2,0:T(8,128)(2,1)S(1)}, u32[]{:S(2)}, u32[]{:S(2)}) collective-permute-start(bf16[2,768,384]{1,2,0:T(8,128)(2,1)} %get-tuple-element.328), channel_id=1, source_target_pairs={{16,0},{32,16},{48,32},{64,48},{80,64},{96,80},{112,96},{128,112},... | collective-permute-start | bytes 3538952 | tf_op jit(solution)/shard_map/while/body/ppermute | solution.py:13
  123.7 19.7 %collective-permute-start = (bf16[2,768,384]{1,2,0:T(8,128)(2,1)}, bf16[2,768,384]{1,2,0:T(8,128)(2,1)S(1)}, u32[]{:S(2)}, u32[]{:S(2)}) collective-permute-start(bf16[2,768,384]{1,2,0:T(8,128)(2,1)} %get-tuple-element.329), channel_id=1, source_target_pairs={{0,16},{16,32},{32,48},{48,64},{64,80},{80,96},{96,112},{112,128},... | collective-permute-start | bytes 3538952 | tf_op jit(solution)/shard_map/while/body/ppermute | solution.py:13
  130.5 9.4 %copy-start.3 = (pred[768,768]{0,1:T(8,128)(4,1)S(1)}, pred[768,768]{0,1:T(8,128)(4,1)}, u32[]{:S(2)}) copy-start(pred[768,768]{0,1:T(8,128)(4,1)} %copy.76) | copy-start | bytes 1769476 | tf_op jit(solution)/shard_map/while
  130.6 9.4 %copy-start.6 = (bf16[1,768,384]{1,2,0:T(8,128)(2,1)S(1)}, bf16[1,768,384]{1,2,0:T(8,128)(2,1)}, u32[]{:S(2)}) copy-start(bf16[1,768,384]{1,2,0:T(8,128)(2,1)} %get-tuple-element.347) | copy-start | bytes 1769476 | tf_op jit(solution)/shard_map/while
  145.5 1.6 copy-start.1
  147.0 0.7 copy-start.7
  147.4 2.5 %copy-start.2 = (f32[768,384]{0,1:T(8,128)}, f32[768,384]{0,1:T(8,128)S(1)}, u32[]{:S(2)}) copy-start(f32[768,384]{0,1:T(8,128)S(1)} %bitcast_add_fusion.3) | copy-start | bytes 3538948 | tf_op jit(solution)/shard_map/while
  147.8 2.1 %copy-start.8 = (f32[3,768]{1,0:T(4,128)}, f32[3,768]{1,0:T(4,128)S(1)}, u32[]{:S(2)}) copy-start(f32[3,768]{1,0:T(4,128)S(1)} %add_add_fusion.2) | copy-start | bytes 27652 | tf_op jit(solution)/shard_map/while
  149.8 18.0 %collective-permute-start.1 = (bf16[2,768,384]{1,2,0:T(8,128)(2,1)}, bf16[2,768,384]{1,2,0:T(8,128)(2,1)S(1)}, u32[]{:S(2)}, u32[]{:S(2)}) collective-permute-start(bf16[2,768,384]{1,2,0:T(8,128)(2,1)} %get-tuple-element.328), channel_id=1, source_target_pairs={{16,0},{32,16},{48,32},{64,48},{80,64},{96,80},{112,96},{128,112},... | collective-permute-start | bytes 3538952 | tf_op jit(solution)/shard_map/while/body/ppermute | solution.py:13
  151.8 19.7 %collective-permute-start = (bf16[2,768,384]{1,2,0:T(8,128)(2,1)}, bf16[2,768,384]{1,2,0:T(8,128)(2,1)S(1)}, u32[]{:S(2)}, u32[]{:S(2)}) collective-permute-start(bf16[2,768,384]{1,2,0:T(8,128)(2,1)} %get-tuple-element.329), channel_id=1, source_target_pairs={{0,16},{16,32},{32,48},{48,64},{64,80},{80,96},{96,112},{112,128},... | collective-permute-start | bytes 3538952 | tf_op jit(solution)/shard_map/while/body/ppermute | solution.py:13
  158.6 9.4 %copy-start.3 = (pred[768,768]{0,1:T(8,128)(4,1)S(1)}, pred[768,768]{0,1:T(8,128)(4,1)}, u32[]{:S(2)}) copy-start(pred[768,768]{0,1:T(8,128)(4,1)} %copy.76) | copy-start | bytes 1769476 | tf_op jit(solution)/shard_map/while
  158.6 9.4 %copy-start.6 = (bf16[1,768,384]{1,2,0:T(8,128)(2,1)S(1)}, bf16[1,768,384]{1,2,0:T(8,128)(2,1)}, u32[]{:S(2)}) copy-start(bf16[1,768,384]{1,2,0:T(8,128)(2,1)} %get-tuple-element.347) | copy-start | bytes 1769476 | tf_op jit(solution)/shard_map/while
  173.5 1.6 copy-start.1
  175.1 0.7 copy-start.7
  175.4 2.5 %copy-start.2 = (f32[768,384]{0,1:T(8,128)}, f32[768,384]{0,1:T(8,128)S(1)}, u32[]{:S(2)}) copy-start(f32[768,384]{0,1:T(8,128)S(1)} %bitcast_add_fusion.3) | copy-start | bytes 3538948 | tf_op jit(solution)/shard_map/while
  175.8 2.1 %copy-start.8 = (f32[3,768]{1,0:T(4,128)}, f32[3,768]{1,0:T(4,128)S(1)}, u32[]{:S(2)}) copy-start(f32[3,768]{1,0:T(4,128)S(1)} %add_add_fusion.2) | copy-start | bytes 27652 | tf_op jit(solution)/shard_map/while
Sparse Core Ops, SparseCore 0:
  9.1 57.1 all-gather.1
where the time goes:
time: 201 us; the launch traced here: 200 us
  waiting for transfers between devices  67.7 us (34%)
  matrix products  41.3 us (21%)
  blocking collectives  24.7 us (12%)
  local copies, waits for them, and re-layouts  24 us (12%)
  starting transfers between devices  16.9 us (8%)
  between operations  14.7 us (7%)
  other arithmetic  10.2 us (5%)
    all_gather x1, waiting for transfers between devices, shards(): piece = lax.all_gather(hidden, 'head', axis=0, tiled=True)  39.2 us
    ppermute x6, waiting for transfers between devices, shifted(): return lax.ppermute(block, axis, route)  27.8 us
    ppermute x6, starting transfers between devices, shifted(): return lax.ppermute(block, axis, route)  16.9 us
    dot_general x3, matrix products, shards(): jnp.dot(piece, qkv_weight[j], preferred_element_type=jnp.float32)  15.3 us
    dot_general x7, matrix products, tile_terms(): jnp.einsum('qhd,khd->hqk', query_h, keys_h, preferred_element_type=jnp.fl...  14 us
    all_to_all x1, blocking collectives, shards(): lax.all_to_all(attended, 'head', split_axis=0, concat_axis=1, tiled=True)  12.7 us
    pmax x1, blocking collectives, shards(): farthest = lax.pmax(jnp.stack([ahead, behind]), 'blk')  12 us
    dot_general x7, matrix products, tile_terms(): jnp.einsum('hqk,khd->qhd', weights.astype(jnp.bfloat16), values_h, prefer...  11.9 us
  transfers between devices with their start and end apart: 7, of which 4 were waited for; matrix products, arithmetic and copies ran while one was open for 13% of the time, Pallas kernels for 0%

commit v1 on v0

--- a/solution.py
+++ b/solution.py
@@ -60,7 +60,8 @@
 
 def shards(hidden, qkv_weight, qkv_bias, norm_gains, tile_lists, tile_counts):
     heads = qkv_weight.shape[2] // HD
-    piece = lax.all_gather(hidden, "head", axis=0, tiled=True)
+    sent = jnp.stack([hidden] * lax.axis_size("head"))
+    piece = jnp.concatenate(lax.all_to_all(sent, "head", 0, 0), axis=0)
     made = [
         jnp.dot(piece, qkv_weight[j], preferred_element_type=jnp.float32)
         + qkv_bias[j].astype(jnp.float32)

time: 201 us -> 191 us (0.950)
  between operations: 14.7 us -> 1.46 us
  waiting for transfers between devices: 67.7 us -> 61.5 us
  starting transfers between devices: 16.9 us -> 23 us
  local copies, waits for them, and re-layouts: 24 us -> 27.4 us
    all_gather x1 -> x0, waiting for transfers between devices: 39.2 us -> none  [shards(): piece = lax.all_gather(hidden, 'head', axis=0, tiled=True)]
    all_to_all x0 -> x1, waiting for transfers between devices: none -> 33.6 us  [shards(): piece = jnp.concatenate(lax.all_to_all(sent, 'head', 0, 0), axis=0)]
    all_to_all x0 -> x1, starting transfers between devices: none -> 5.06 us  [shards(): piece = jnp.concatenate(lax.all_to_all(sent, 'head', 0, 0), axis=0)]
    another operation x0 -> x1, local copies, waits for them, and re-layouts: none -> 4.04 us  [shards(): sent = jnp.stack([hidden] * lax.axis_size('head'))]
    while x42 -> x48, local copies, waits for them, and re-layouts: 7.32 us -> 7.31 us
  transfers between devices with their start and end apart: 7 -> 7, of which waited for: 4 -> 4; matrix products, arithmetic and copies ran while one was open for 13% -> 14% of each run, Pallas kernels for 0% -> 0%
where the time goes in v1:
time: 191 us; the launch traced here: 189 us
  waiting for transfers between devices  61.5 us (32%)
  matrix products  41.7 us (22%)
  local copies, waits for them, and re-layouts  27.4 us (14%)
  blocking collectives  24.3 us (13%)
  starting transfers between devices  23 us (12%)
  other arithmetic  9.49 us (5%)
    all_to_all x1, waiting for transfers between devices, shards(): piece = jnp.concatenate(lax.all_to_all(sent, 'head', 0, 0), axis=0)  33.6 us
    ppermute x6, waiting for transfers between devices, shifted(): return lax.ppermute(block, axis, route)  27.8 us
    ppermute x6, starting transfers between devices, shifted(): return lax.ppermute(block, axis, route)  18 us
    dot_general x3, matrix products, shards(): jnp.dot(piece, qkv_weight[j], preferred_element_type=jnp.float32)  15.3 us
    dot_general x7, matrix products, tile_terms(): jnp.einsum('qhd,khd->hqk', query_h, keys_h, preferred_element_type=jnp.fl...  14.2 us
    pmax x1, blocking collectives, shards(): farthest = lax.pmax(jnp.stack([ahead, behind]), 'blk')  12.8 us
    dot_general x7, matrix products, tile_terms(): jnp.einsum('hqk,khd->qhd', weights.astype(jnp.bfloat16), values_h, prefer...  12.2 us
    all_to_all x1, blocking collectives, shards(): lax.all_to_all(attended, 'head', split_axis=0, concat_axis=1, tiled=True)  11.4 us
  transfers between devices with their start and end apart: 7, of which 4 were waited for; matrix products, arithmetic and copies ran while one was open for 14% of the time, Pallas kernels for 0%

profile of v1, /device:TPU:65, one launch (start us, length us, event | category | flops | bytes accessed | tf_op | source)
XLA Modules:
  0.0 189.3 jit_solution(1933894426212886928)
XLA Ops:
  0.0 4.0 %stack.24 = bf16[4,192,3072]{2,1,0:T(8,128)(2,1)} broadcast(bf16[192,3072]{1,0:T(8,128)(2,1)} %param.8), dimensions={1,2} | broadcast | bytes 5898240 | tf_op jit(solution)/shard_map/stack | solution.py:63
  4.0 5.1 %all-to-all-start = ((bf16[4,192,3072]{2,1,0:T(8,128)(2,1)}), bf16[4,192,3072]{2,1,0:T(8,128)(2,1)}, u32[]{:S(2)}, u32[]{:S(2)}) async-start(bf16[4,192,3072]{2,1,0:T(8,128)(2,1)} %stack.24), calls=%async_computation | async-start | bytes 9437184 | tf_op jit(solution)/shard_map/all_to_all | solution.py:64
  10.1 1.3 pad_add_fusion
  11.4 12.8 %pmax.7 = s32[2]{0:T(128)S(1)} all-reduce(s32[2]{0:T(128)S(1)} %pad_add_fusion), channel_id=1, replica_groups=mesh['blk'=16,'head'=4,'dp'=4] {'blk'}, use_global_device_ids=true, to_apply=%region_6.7 | all-reduce | flops 2 | bytes 16 | tf_op jit(solution)/shard_map/pmax | solution.py:88
  24.6 1.6 copy.56
  29.4 33.6 %all-to-all-done = bf16[4,192,3072]{2,1,0:T(8,128)(2,1)} async-done(((bf16[4,192,3072]{2,1,0:T(8,128)(2,1)}), bf16[4,192,3072]{2,1,0:T(8,128)(2,1)}, u32[]{:S(2)}, u32[]{:S(2)}) %all-to-all-start) | async-done | bytes 4718624 | tf_op jit(solution)/shard_map/all_to_all | solution.py:64
  63.0 5.1 %fusion.60 = (f32[768,384]{0,1:T(8,128)S(1)}, f32[768,384]{0,1:T(8,128)S(1)}) fusion(f32[384]{0:T(512)S(1)} %get-tuple-element.181, bf16[768,3072]{1,0:T(8,128)(2,1)} %bitcast.12, bf16[3,3072,384]{2,1,0:T(8,128)(2,1)} %param.9), kind=kOutput, calls=%fused_computation.93 | convolution fusion | flops 1812529152 | bytes 9438720 | tf_op jit(solution)/shard_map/dot_general | solution.py:66
  68.9 5.1 %fusion.59 = (f32[768,384]{0,1:T(8,128)S(1)}, f32[768,384]{0,1:T(8,128)S(1)}) fusion(f32[384]{0:T(512)} %get-tuple-element.180, bf16[768,3072]{1,0:T(8,128)(2,1)} %bitcast.12, bf16[3,3072,384]{2,1,0:T(8,128)(2,1)} %param.9), kind=kOutput, calls=%fused_computation.92 | convolution fusion | flops 1812529152 | bytes 9439232 | tf_op jit(solution)/shard_map/dot_general | solution.py:66
  75.4 5.1 %fusion.45 = bf16[768,384]{0,1:T(8,128)(2,1)S(1)} fusion(bf16[768,3072]{1,0:T(8,128)(2,1)} %bitcast.12, bf16[3,3072,384]{2,1,0:T(8,128)(2,1)} %param.9, f32[384]{0:T(512)} %get-tuple-element.179), kind=kOutput, calls=%fused_computation.53 | convolution fusion | flops 1812529152 | bytes 7669760 | tf_op jit(solution)/shard_map/dot_general | solution.py:66
  80.7 1.1 pad_maximum_fusion
  81.8 2.5 %copy.81 = bf16[2,768,384]{1,2,0:T(8,128)(2,1)} copy(bf16[2,768,384]{1,2,0:T(8,128)(2,1)} %pad_maximum_fusion) | data formatting | bytes 2359296
  84.5 2.5 %fusion.21 = (f32[3,768]{1,0:T(4,128)}, f32[3,768,768]{1,2,0:T(8,128)S(1)}) fusion(pred[768,768]{0,1:T(8,128)(4,1)S(1)} %copy-done.4, bf16[768,3,128]{0,2,1:T(8,128)(2,1)S(1)} %bitcast.139, bf16[768,3,128]{0,2,1:T(8,128)(2,1)S(1)} %bitcast.136), kind=kOutput, calls=%fused_computation.36 | convolution fusion | flops 458290944 | bytes 8856576 | tf_op jit(solution)/shard_map/qhd,khd->hqk/dot_general | solution.py:36
  87.0 2.6 %fusion.22 = f32[3,128,768]{2,1,0:T(8,128)} fusion(bf16[768,3,128]{0,2,1:T(8,128)(2,1)S(1)} %bitcast.144, f32[3,768,768]{1,2,0:T(8,128)S(1)} %get-tuple-element.223, pred[768,768]{0,1:T(8,128)(4,1)S(1)} %copy-done.4), kind=kOutput, calls=%fused_computation.37 | convolution fusion | flops 458293248 | bytes 9437184 | tf_op jit(solution)/shard_map/hqk,khd->qhd/dot_general | solution.py:44
  89.6 85.8 %while.19 = (s32[]{:T(128)}, f32[3,768]{1,0:T(4,128)}, f32[768,384]{0,1:T(8,128)}, bf16[2,768,384]{1,2,0:T(8,128)(2,1)}, bf16[2,768,384]{1,2,0:T(8,128)(2,1)}, /...) while((s32[]{:T(128)}, f32[3,768]{1,0:T(4,128)}, ...), condition=%wide.region_12.13_spmd, body=%wide.region_7.12_spmd.sunk | while | flops 1833884160 | bytes 78004888 | solution.py:104
  89.6 3.4 %collective-permute-start.1 = (bf16[2,768,384]{1,2,0:T(8,128)(2,1)}, bf16[2,768,384]{1,2,0:T(8,128)(2,1)S(1)}, u32[]{:S(2)}, u32[]{:S(2)}) collective-permute-start(bf16[2,768,384]{1,2,0:T(8,128)(2,1)} %get-tuple-element.328), channel_id=1, source_target_pairs={{16,0},{32,16},{48,32},{64,48},{80,64},{96,80},{112,96},{128,112},... | collective-permute-start | bytes 3538952 | tf_op jit(solution)/shard_map/while/body/ppermute | solution.py:13
  93.0 3.4 %collective-permute-start = (bf16[2,768,384]{1,2,0:T(8,128)(2,1)}, bf16[2,768,384]{1,2,0:T(8,128)(2,1)S(1)}, u32[]{:S(2)}, u32[]{:S(2)}) collective-permute-start(bf16[2,768,384]{1,2,0:T(8,128)(2,1)} %get-tuple-element.329), channel_id=1, source_target_pairs={{0,16},{16,32},{32,48},{48,64},{64,80},{80,96},{96,112},{112,128},... | collective-permute-start | bytes 3538952 | tf_op jit(solution)/shard_map/while/body/ppermute | solution.py:13
  96.9 1.6 copy.76
  98.6 1.0 copy.75
  99.7 9.3 %collective-permute-done.1 = bf16[2,768,384]{1,2,0:T(8,128)(2,1)S(1)} collective-permute-done((bf16[2,768,384]{1,2,0:T(8,128)(2,1)}, bf16[2,768,384]{1,2,0:T(8,128)(2,1)S(1)}, u32[]{:S(2)}, u32[]{:S(2)}) %collective-permute-start.1) | collective-permute-done | bytes 1179680 | tf_op jit(solution)/shard_map/while/body/ppermute | solution.py:13
  109.0 2.0 %fusion.98 = (f32[3,768]{1,0:T(4,128)S(1)}, f32[3,768,768]{1,2,0:T(8,128)S(1)}) fusion(pred[768,768]{0,1:T(8,128)(4,1)S(1)} %copy-done.3, bf16[768,3,128]{0,2,1:T(8,128)(2,1)S(1)} %bitcast.141, bf16[768,3,128]{0,2,1:T(8,128)(2,1)S(1)} %bitcast.130), kind=kOutput, calls=%fused_computation.3.clone.1 | convolution fusion | flops 458290944 | bytes 8856576 | tf_op jit(solution)/shard_map/while/body/qhd,khd->hqk/dot_general | solution.py:36
  111.0 1.6 fusion.100
  112.7 1.9 %fusion.96 = (f32[3,768]{1,0:T(4,128)S(1)}, f32[3,768,768]{1,2,0:T(8,128)S(1)}) fusion(pred[768,768]{0,1:T(8,128)(4,1)S(1)} %copy.75, bf16[768,3,128]{0,2,1:T(8,128)(2,1)S(1)} %bitcast.142, bf16[768,3,128]{0,2,1:T(8,128)(2,1)S(1)} %bitcast.131), kind=kOutput, calls=%fused_computation.5.clone.1 | convolution fusion | flops 458290944 | bytes 8856576 | tf_op jit(solution)/shard_map/while/body/qhd,khd->hqk/dot_general | solution.py:36
  114.6 1.6 fusion.99
  117.0 1.0 copy.90
  118.0 1.0 copy.91
  119.0 1.9 %collective-permute-start.1 = (bf16[2,768,384]{1,2,0:T(8,128)(2,1)}, bf16[2,768,384]{1,2,0:T(8,128)(2,1)S(1)}, u32[]{:S(2)}, u32[]{:S(2)}) collective-permute-start(bf16[2,768,384]{1,2,0:T(8,128)(2,1)} %get-tuple-element.328), channel_id=1, source_target_pairs={{16,0},{32,16},{48,32},{64,48},{80,64},{96,80},{112,96},{128,112},... | collective-permute-start | bytes 3538952 | tf_op jit(solution)/shard_map/while/body/ppermute | solution.py:13
  121.0 3.6 %collective-permute-start = (bf16[2,768,384]{1,2,0:T(8,128)(2,1)}, bf16[2,768,384]{1,2,0:T(8,128)(2,1)S(1)}, u32[]{:S(2)}, u32[]{:S(2)}) collective-permute-start(bf16[2,768,384]{1,2,0:T(8,128)(2,1)} %get-tuple-element.329), channel_id=1, source_target_pairs={{0,16},{16,32},{32,48},{48,64},{64,80},{80,96},{96,112},{112,128},... | collective-permute-start | bytes 3538952 | tf_op jit(solution)/shard_map/while/body/ppermute | solution.py:13
  125.0 1.6 copy.76
  126.7 1.0 copy.75
  127.8 9.3 %collective-permute-done.1 = bf16[2,768,384]{1,2,0:T(8,128)(2,1)S(1)} collective-permute-done((bf16[2,768,384]{1,2,0:T(8,128)(2,1)}, bf16[2,768,384]{1,2,0:T(8,128)(2,1)S(1)}, u32[]{:S(2)}, u32[]{:S(2)}) %collective-permute-start.1) | collective-permute-done | bytes 1179680 | tf_op jit(solution)/shard_map/while/body/ppermute | solution.py:13
  137.2 2.0 %fusion.98 = (f32[3,768]{1,0:T(4,128)S(1)}, f32[3,768,768]{1,2,0:T(8,128)S(1)}) fusion(pred[768,768]{0,1:T(8,128)(4,1)S(1)} %copy-done.3, bf16[768,3,128]{0,2,1:T(8,128)(2,1)S(1)} %bitcast.141, bf16[768,3,128]{0,2,1:T(8,128)(2,1)S(1)} %bitcast.130), kind=kOutput, calls=%fused_computation.3.clone.1 | convolution fusion | flops 458290944 | bytes 8856576 | tf_op jit(solution)/shard_map/while/body/qhd,khd->hqk/dot_general | solution.py:36
  139.1 1.6 fusion.100
  140.9 1.9 %fusion.96 = (f32[3,768]{1,0:T(4,128)S(1)}, f32[3,768,768]{1,2,0:T(8,128)S(1)}) fusion(pred[768,768]{0,1:T(8,128)(4,1)S(1)} %copy.75, bf16[768,3,128]{0,2,1:T(8,128)(2,1)S(1)} %bitcast.142, bf16[768,3,128]{0,2,1:T(8,128)(2,1)S(1)} %bitcast.131), kind=kOutput, calls=%fused_computation.5.clone.1 | convolution fusion | flops 458290944 | bytes 8856576 | tf_op jit(solution)/shard_map/while/body/qhd,khd->hqk/dot_general | solution.py:36
  142.8 1.6 fusion.99
  145.1 1.0 copy.90
  146.1 1.0 copy.91
  147.2 1.9 %collective-permute-start.1 = (bf16[2,768,384]{1,2,0:T(8,128)(2,1)}, bf16[2,768,384]{1,2,0:T(8,128)(2,1)S(1)}, u32[]{:S(2)}, u32[]{:S(2)}) collective-permute-start(bf16[2,768,384]{1,2,0:T(8,128)(2,1)} %get-tuple-element.328), channel_id=1, source_target_pairs={{16,0},{32,16},{48,32},{64,48},{80,64},{96,80},{112,96},{128,112},... | collective-permute-start | bytes 3538952 | tf_op jit(solution)/shard_map/while/body/ppermute | solution.py:13
  149.1 3.6 %collective-permute-start = (bf16[2,768,384]{1,2,0:T(8,128)(2,1)}, bf16[2,768,384]{1,2,0:T(8,128)(2,1)S(1)}, u32[]{:S(2)}, u32[]{:S(2)}) collective-permute-start(bf16[2,768,384]{1,2,0:T(8,128)(2,1)} %get-tuple-element.329), channel_id=1, source_target_pairs={{0,16},{16,32},{32,48},{48,64},{64,80},{80,96},{96,112},{112,128},... | collective-permute-start | bytes 3538952 | tf_op jit(solution)/shard_map/while/body/ppermute | solution.py:13
  153.2 1.6 copy.76
  154.9 1.0 copy.75
  155.9 9.3 %collective-permute-done.1 = bf16[2,768,384]{1,2,0:T(8,128)(2,1)S(1)} collective-permute-done((bf16[2,768,384]{1,2,0:T(8,128)(2,1)}, bf16[2,768,384]{1,2,0:T(8,128)(2,1)S(1)}, u32[]{:S(2)}, u32[]{:S(2)}) %collective-permute-start.1) | collective-permute-done | bytes 1179680 | tf_op jit(solution)/shard_map/while/body/ppermute | solution.py:13
  165.3 2.0 %fusion.98 = (f32[3,768]{1,0:T(4,128)S(1)}, f32[3,768,768]{1,2,0:T(8,128)S(1)}) fusion(pred[768,768]{0,1:T(8,128)(4,1)S(1)} %copy-done.3, bf16[768,3,128]{0,2,1:T(8,128)(2,1)S(1)} %bitcast.141, bf16[768,3,128]{0,2,1:T(8,128)(2,1)S(1)} %bitcast.130), kind=kOutput, calls=%fused_computation.3.clone.1 | convolution fusion | flops 458290944 | bytes 8856576 | tf_op jit(solution)/shard_map/while/body/qhd,khd->hqk/dot_general | solution.py:36
  167.3 1.6 fusion.100
  169.0 1.9 %fusion.96 = (f32[3,768]{1,0:T(4,128)S(1)}, f32[3,768,768]{1,2,0:T(8,128)S(1)}) fusion(pred[768,768]{0,1:T(8,128)(4,1)S(1)} %copy.75, bf16[768,3,128]{0,2,1:T(8,128)(2,1)S(1)} %bitcast.142, bf16[768,3,128]{0,2,1:T(8,128)(2,1)S(1)} %bitcast.131), kind=kOutput, calls=%fused_computation.5.clone.1 | convolution fusion | flops 458290944 | bytes 8856576 | tf_op jit(solution)/shard_map/while/body/qhd,khd->hqk/dot_general | solution.py:36
  170.9 1.6 fusion.99
  174.3 1.0 copy.91
  175.4 1.4 fusion.48
  177.0 11.4 %all_to_all.24 = bf16[4,192,384]{2,1,0:T(8,128)(2,1)S(1)} all-to-all(bf16[4,192,384]{2,1,0:T(8,128)(2,1)S(1)} %bitcast.133), channel_id=1, replica_groups=mesh['blk'=16,'head'=4,'dp'=4] {'head'}, dimensions={0} | all-to-all | bytes 1179648 | tf_op jit(solution)/shard_map/all_to_all | solution.py:111
  (113 shorter events, 12.1 us)
Async XLA Ops:
  0.0 9.1 %copy-start = (s32[32,12]{0,1:T(8,128)S(1)}, s32[32,12]{0,1:T(8,128)}, u32[]{:S(2)}) copy-start(s32[32,12]{0,1:T(8,128)} %param.12) | copy-start | bytes 4612
  4.0 5.3 %copy-start.16 = (s32[32]{0:T(128)S(1)}, s32[32]{0:T(128)}, u32[]{:S(2)}) copy-start(s32[32]{0:T(128)} %param.13) | copy-start | bytes 388
  4.0 24.1 %copy-start.11 = (bf16[3,384]{1,0:T(4,128)(2,1)S(1)}, bf16[3,384]{1,0:T(4,128)(2,1)}, u32[]{:S(2)}) copy-start(bf16[3,384]{1,0:T(4,128)(2,1)} %param.10) | copy-start | bytes 6916
  4.0 24.7 %copy-start.12 = (f32[2,128]{1,0:T(2,128)S(1)}, f32[2,128]{1,0:T(2,128)}, u32[]{:S(2)}) copy-start(f32[2,128]{1,0:T(2,128)} %param.11) | copy-start | bytes 3076
  4.0 59.0 %all-to-all-start = ((bf16[4,192,3072]{2,1,0:T(8,128)(2,1)}), bf16[4,192,3072]{2,1,0:T(8,128)(2,1)}, u32[]{:S(2)}, u32[]{:S(2)}) async-start(bf16[4,192,3072]{2,1,0:T(8,128)(2,1)} %stack.24), calls=%async_computation | async-start | bytes 9437184 | tf_op jit(solution)/shard_map/all_to_all | solution.py:64
  9.4 15.0 %copy-start.13 = (s32[2]{0:T(128)}, s32[2]{0:T(128)S(1)}, u32[]{:S(2)}) copy-start(s32[2]{0:T(128)S(1)} %dynamic_slice.7) | copy-start | bytes 28
  75.4 5.1 %copy-start.9 = (f32[768,3]{0,1:T(4,128)S(1)}, f32[768,3]{0,1:T(4,128)}, u32[]{:S(2)}) copy-start(f32[768,3]{0,1:T(4,128)} %add_rsqrt_fusion) | copy-start | bytes 27652
  75.4 5.1 %copy-start.10 = (f32[384]{0:T(512)S(1)}, f32[384]{0:T(512)}, u32[]{:S(2)}) copy-start(f32[384]{0:T(512)} %get-tuple-element.224) | copy-start | bytes 4612
  81.8 2.7 %copy-start.4 = (pred[768,768]{0,1:T(8,128)(4,1)S(1)}, pred[768,768]{0,1:T(8,128)(4,1)}, u32[]{:S(2)}) copy-start(pred[768,768]{0,1:T(8,128)(4,1)} %copy.56) | copy-start | bytes 1769476
  84.5 2.5 %copy-start.5 = (bf16[768,384]{0,1:T(8,128)(2,1)}, bf16[768,384]{0,1:T(8,128)(2,1)S(1)}, u32[]{:S(2)}) copy-start(bf16[768,384]{0,1:T(8,128)(2,1)S(1)} %fusion.52) | copy-start | bytes 1769476
  87.0 2.6 %copy-start.14 = (s32[2]{0:T(128)S(1)}, s32[2]{0:T(128)}, u32[]{:S(2)}) copy-start(s32[2]{0:T(128)} %copy-done.13) | copy-start | bytes 28
  89.6 19.3 %collective-permute-start.1 = (bf16[2,768,384]{1,2,0:T(8,128)(2,1)}, bf16[2,768,384]{1,2,0:T(8,128)(2,1)S(1)}, u32[]{:S(2)}, u32[]{:S(2)}) collective-permute-start(bf16[2,768,384]{1,2,0:T(8,128)(2,1)} %get-tuple-element.328), channel_id=1, source_target_pairs={{16,0},{32,16},{48,32},{64,48},{80,64},{96,80},{112,96},{128,112},... | collective-permute-start | bytes 3538952 | tf_op jit(solution)/shard_map/while/body/ppermute | solution.py:13
  93.0 19.6 %collective-permute-start = (bf16[2,768,384]{1,2,0:T(8,128)(2,1)}, bf16[2,768,384]{1,2,0:T(8,128)(2,1)S(1)}, u32[]{:S(2)}, u32[]{:S(2)}) collective-permute-start(bf16[2,768,384]{1,2,0:T(8,128)(2,1)} %get-tuple-element.329), channel_id=1, source_target_pairs={{0,16},{16,32},{32,48},{48,64},{64,80},{80,96},{96,112},{112,128},... | collective-permute-start | bytes 3538952 | tf_op jit(solution)/shard_map/while/body/ppermute | solution.py:13
  99.6 9.4 %copy-start.3 = (pred[768,768]{0,1:T(8,128)(4,1)S(1)}, pred[768,768]{0,1:T(8,128)(4,1)}, u32[]{:S(2)}) copy-start(pred[768,768]{0,1:T(8,128)(4,1)} %copy.76) | copy-start | bytes 1769476 | tf_op jit(solution)/shard_map/while
  99.6 9.4 %copy-start.6 = (bf16[1,768,384]{1,2,0:T(8,128)(2,1)S(1)}, bf16[1,768,384]{1,2,0:T(8,128)(2,1)}, u32[]{:S(2)}) copy-start(bf16[1,768,384]{1,2,0:T(8,128)(2,1)} %get-tuple-element.347) | copy-start | bytes 1769476 | tf_op jit(solution)/shard_map/while
  114.6 1.6 copy-start.1
  116.2 0.7 copy-start.7
  116.6 2.5 %copy-start.2 = (f32[768,384]{0,1:T(8,128)}, f32[768,384]{0,1:T(8,128)S(1)}, u32[]{:S(2)}) copy-start(f32[768,384]{0,1:T(8,128)S(1)} %bitcast_add_fusion.3) | copy-start | bytes 3538948 | tf_op jit(solution)/shard_map/while
  117.0 2.1 %copy-start.8 = (f32[3,768]{1,0:T(4,128)}, f32[3,768]{1,0:T(4,128)S(1)}, u32[]{:S(2)}) copy-start(f32[3,768]{1,0:T(4,128)S(1)} %add_add_fusion.2) | copy-start | bytes 27652 | tf_op jit(solution)/shard_map/while
  117.0 2.1 %copy-start.15 = (s32[2]{0:T(128)S(1)}, s32[2]{0:T(128)}, u32[]{:S(2)}) copy-start(s32[2]{0:T(128)} %get-tuple-element.368) | copy-start | bytes 28 | tf_op jit(solution)/shard_map/while
  119.0 18.0 %collective-permute-start.1 = (bf16[2,768,384]{1,2,0:T(8,128)(2,1)}, bf16[2,768,384]{1,2,0:T(8,128)(2,1)S(1)}, u32[]{:S(2)}, u32[]{:S(2)}) collective-permute-start(bf16[2,768,384]{1,2,0:T(8,128)(2,1)} %get-tuple-element.328), channel_id=1, source_target_pairs={{16,0},{32,16},{48,32},{64,48},{80,64},{96,80},{112,96},{128,112},... | collective-permute-start | bytes 3538952 | tf_op jit(solution)/shard_map/while/body/ppermute | solution.py:13
  121.0 19.8 %collective-permute-start = (bf16[2,768,384]{1,2,0:T(8,128)(2,1)}, bf16[2,768,384]{1,2,0:T(8,128)(2,1)S(1)}, u32[]{:S(2)}, u32[]{:S(2)}) collective-permute-start(bf16[2,768,384]{1,2,0:T(8,128)(2,1)} %get-tuple-element.329), channel_id=1, source_target_pairs={{0,16},{16,32},{32,48},{48,64},{64,80},{80,96},{96,112},{112,128},... | collective-permute-start | bytes 3538952 | tf_op jit(solution)/shard_map/while/body/ppermute | solution.py:13
  127.8 9.4 %copy-start.3 = (pred[768,768]{0,1:T(8,128)(4,1)S(1)}, pred[768,768]{0,1:T(8,128)(4,1)}, u32[]{:S(2)}) copy-start(pred[768,768]{0,1:T(8,128)(4,1)} %copy.76) | copy-start | bytes 1769476 | tf_op jit(solution)/shard_map/while
  127.8 9.4 %copy-start.6 = (bf16[1,768,384]{1,2,0:T(8,128)(2,1)S(1)}, bf16[1,768,384]{1,2,0:T(8,128)(2,1)}, u32[]{:S(2)}) copy-start(bf16[1,768,384]{1,2,0:T(8,128)(2,1)} %get-tuple-element.347) | copy-start | bytes 1769476 | tf_op jit(solution)/shard_map/while
  142.8 1.6 copy-start.1
  144.4 0.7 copy-start.7
  144.7 2.5 %copy-start.2 = (f32[768,384]{0,1:T(8,128)}, f32[768,384]{0,1:T(8,128)S(1)}, u32[]{:S(2)}) copy-start(f32[768,384]{0,1:T(8,128)S(1)} %bitcast_add_fusion.3) | copy-start | bytes 3538948 | tf_op jit(solution)/shard_map/while
  145.1 2.1 %copy-start.8 = (f32[3,768]{1,0:T(4,128)}, f32[3,768]{1,0:T(4,128)S(1)}, u32[]{:S(2)}) copy-start(f32[3,768]{1,0:T(4,128)S(1)} %add_add_fusion.2) | copy-start | bytes 27652 | tf_op jit(solution)/shard_map/while
  145.1 2.1 %copy-start.15 = (s32[2]{0:T(128)S(1)}, s32[2]{0:T(128)}, u32[]{:S(2)}) copy-start(s32[2]{0:T(128)} %get-tuple-element.368) | copy-start | bytes 28 | tf_op jit(solution)/shard_map/while
  147.2 18.0 %collective-permute-start.1 = (bf16[2,768,384]{1,2,0:T(8,128)(2,1)}, bf16[2,768,384]{1,2,0:T(8,128)(2,1)S(1)}, u32[]{:S(2)}, u32[]{:S(2)}) collective-permute-start(bf16[2,768,384]{1,2,0:T(8,128)(2,1)} %get-tuple-element.328), channel_id=1, source_target_pairs={{16,0},{32,16},{48,32},{64,48},{80,64},{96,80},{112,96},{128,112},... | collective-permute-start | bytes 3538952 | tf_op jit(solution)/shard_map/while/body/ppermute | solution.py:13
  149.1 19.8 %collective-permute-start = (bf16[2,768,384]{1,2,0:T(8,128)(2,1)}, bf16[2,768,384]{1,2,0:T(8,128)(2,1)S(1)}, u32[]{:S(2)}, u32[]{:S(2)}) collective-permute-start(bf16[2,768,384]{1,2,0:T(8,128)(2,1)} %get-tuple-element.329), channel_id=1, source_target_pairs={{0,16},{16,32},{32,48},{48,64},{64,80},{80,96},{96,112},{112,128},... | collective-permute-start | bytes 3538952 | tf_op jit(solution)/shard_map/while/body/ppermute | solution.py:13
  155.9 9.4 %copy-start.3 = (pred[768,768]{0,1:T(8,128)(4,1)S(1)}, pred[768,768]{0,1:T(8,128)(4,1)}, u32[]{:S(2)}) copy-start(pred[768,768]{0,1:T(8,128)(4,1)} %copy.76) | copy-start | bytes 1769476 | tf_op jit(solution)/shard_map/while
  155.9 9.4 %copy-start.6 = (bf16[1,768,384]{1,2,0:T(8,128)(2,1)S(1)}, bf16[1,768,384]{1,2,0:T(8,128)(2,1)}, u32[]{:S(2)}) copy-start(bf16[1,768,384]{1,2,0:T(8,128)(2,1)} %get-tuple-element.347) | copy-start | bytes 1769476 | tf_op jit(solution)/shard_map/while
  170.9 1.6 copy-start.1
  172.5 0.7 copy-start.7
  172.9 2.5 %copy-start.2 = (f32[768,384]{0,1:T(8,128)}, f32[768,384]{0,1:T(8,128)S(1)}, u32[]{:S(2)}) copy-start(f32[768,384]{0,1:T(8,128)S(1)} %bitcast_add_fusion.3) | copy-start | bytes 3538948 | tf_op jit(solution)/shard_map/while
  173.3 2.1 %copy-start.8 = (f32[3,768]{1,0:T(4,128)}, f32[3,768]{1,0:T(4,128)S(1)}, u32[]{:S(2)}) copy-start(f32[3,768]{1,0:T(4,128)S(1)} %add_add_fusion.2) | copy-start | bytes 27652 | tf_op jit(solution)/shard_map/while
  173.3 2.1 %copy-start.15 = (s32[2]{0:T(128)S(1)}, s32[2]{0:T(128)}, u32[]{:S(2)}) copy-start(s32[2]{0:T(128)} %get-tuple-element.368) | copy-start | bytes 28 | tf_op jit(solution)/shard_map/while
